TPU v7x, 32 devices: a whole 2x2x4 slice. The times are simulated.
32 devices in a mesh: video: 2 (over y), rows: 4 (over z), cols: 4 (over x, core).
Axes of the slice: x: 2, y: 2, z: 4, core: 2. Of those that a mesh axis runs over, the one named last changes fastest.
Arguments:
- frame_in: bfloat16 [64, 80, 512], P(('video', 'rows'), 'cols'), parts along dimension 0, may hold values from -6 to 6
- norm_gain: float32 [512], replicated, may hold values from 0.5 to 1.5
- w_query: bfloat16 [512, 512], replicated, may hold values from -2 to 2
- w_key: bfloat16 [512, 512], replicated, may hold values from -0.125 to 0.125
- w_value: bfloat16 [512, 512], replicated, may hold values from -0.25 to 0.25
- w_out: bfloat16 [512, 512], replicated, may hold values from -0.25 to 0.25
- conv_gain: float32 [512], replicated, may hold values from 0.5 to 1.5
- conv_cache: bfloat16 [2, 64, 80, 512], P(None, ('video', 'rows'), 'cols'), parts along dimension 1, may hold values from -6 to 6
- w_conv: bfloat16 [3, 3, 3, 512, 256], replicated, may hold values from -0.0546875 to 0.0546875
- conv_bias: float32 [256], replicated, may hold values from -0.5 to 0.5
Outputs:
- hidden: bfloat16 [64, 80, 512], P(('video', 'rows'), 'cols'), parts along dimension 0
- mixed_out: bfloat16 [64, 80, 256], P(('video', 'rows'), 'cols'), parts along dimension 0
There are 2 independent parts, one for each index of `video`. A program takes and returns all parts, laid end to end along the dimension named above; an argument that names none is the same for every part. Nothing has to cross between parts.
All inputs are finite; a program needn't handle non-finite values.
Results may differ from a plain program's by a relative error of at most 0.012.
Values may be sent and summed in bfloat16 or wider, within the bound.
No kernel may reach another device: no remote copies, remote signals or barrier semaphores. Data moves between devices by JAX's collectives and lax.ppermute only.
A program may use at most 128 MiB of HBM per device.

v0:
```python
import math
import jax
import jax.numpy as jnp
from jax import lax
from jax.sharding import PartitionSpec as P


def padded_2(value, sides, width):
    for axis, dim in sides:
        size, length = (lax.axis_size(axis), value.shape[dim])
        up = [(i, (i + 1) % size) for i in range(size - 1)]
        down = [(j, i) for i, j in up]
        last = lax.slice_in_dim(value, length - width, length, axis=dim)
        first = lax.slice_in_dim(value, 0, width, axis=dim)
        before = lax.ppermute(last, axis, up)
        after = lax.ppermute(first, axis, down)
        value = jnp.concatenate([before, value, after], axis=dim)
    return value


def rms_scaled(values, gain):
    mean_sq = jnp.mean(values * values, axis=-1, keepdims=True)
    return values * lax.rsqrt(mean_sq + 1e-06) * gain


def fold_block(running_state, query_keys, block_rows):
    running, total_sum, accumulated = running_state
    scores = lax.dot_general(
        query_keys, block_rows, (((1,), (1,)), ((), ())), preferred_element_type=jnp.float32
    )
    new_max = jnp.maximum(running, jnp.max(scores, axis=1))
    weights = jnp.exp(scores - new_max[:, None])
    total_sum = jnp.sum(weights, axis=1)
    accumulated = jnp.dot(
        weights.astype(jnp.bfloat16), block_rows, preferred_element_type=jnp.float32
    )
    return (new_max, total_sum, accumulated)


def start_for(query_count, channels):
    return (
        jnp.full((query_count,), -1e30, jnp.float32),
        jnp.zeros((query_count,), jnp.float32),
        jnp.zeros((query_count, channels), jnp.float32),
    )


def body(
    frame_in, norm_gain, w_query, w_key, w_value, w_out, conv_gain, conv_cache, w_conv, conv_bias
):
    tile_rows, tile_cols, channels = frame_in.shape
    out_channels = w_conv.shape[4]
    count = tile_rows * tile_cols
    cache_padded = padded_2(conv_cache, (("rows", 1), ("cols", 2)), 1)
    tokens = frame_in.astype(jnp.float32).reshape(count, channels)
    normed = rms_scaled(tokens, norm_gain).astype(jnp.bfloat16)
    query_rows = (
        jnp.dot(normed, w_query, preferred_element_type=jnp.float32) * (1.0 / math.sqrt(channels))
    ).astype(jnp.bfloat16)
    query_keys = jnp.dot(query_rows, w_key.T, preferred_element_type=jnp.float32).astype(
        jnp.bfloat16
    )
    final_state = fold_block(
        start_for(count, channels),
        query_keys,
        lax.all_gather(normed, ("rows", "cols"), axis=0, tiled=True),
    )
    pooled = (final_state[2] / final_state[1][:, None]).astype(jnp.bfloat16)
    attended = jnp.dot(pooled, w_value, preferred_element_type=jnp.float32).astype(jnp.bfloat16)
    hidden = (tokens + jnp.dot(attended, w_out, preferred_element_type=jnp.float32)).astype(
        jnp.bfloat16
    )
    conv_input = jax.nn.silu(rms_scaled(hidden.astype(jnp.float32), conv_gain)).astype(jnp.bfloat16)
    conv_input = conv_input.reshape(1, tile_rows, tile_cols, channels)
    frame_padded = padded_2(conv_input, (("rows", 1), ("cols", 2)), 1)
    padded = jnp.concatenate([cache_padded, frame_padded], axis=0)
    windows = [
        padded[time_off, row_off : row_off + tile_rows, col_off : col_off + tile_cols, :]
        for time_off in range(3)
        for row_off in range(3)
        for col_off in range(3)
    ]
    patches = jnp.concatenate(windows, axis=-1).reshape(count, 27 * channels)
    kernel_rows = w_conv.reshape(27 * channels, out_channels)
    result_sum = hidden[:, :out_channels].astype(jnp.float32) + conv_bias
    result_sum = result_sum + jnp.dot(patches, kernel_rows, preferred_element_type=jnp.float32)
    hidden_out = hidden.reshape(tile_rows, tile_cols, channels)
    mixed_out = result_sum.astype(jnp.bfloat16).reshape(tile_rows, tile_cols, out_channels)
    return (hidden_out, mixed_out)


def solution(mesh):
    in_specs = (
        P(("video", "rows"), "cols", None),
        P(),
        P(),
        P(),
        P(),
        P(),
        P(),
        P(None, ("video", "rows"), "cols", None),
        P(),
        P(),
    )
    out_specs = (P(("video", "rows"), "cols", None), P(("video", "rows"), "cols", None))
    return jax.shard_map(body, mesh=mesh, in_specs=in_specs, out_specs=out_specs, check_vma=False)
```

profile of v0, /device:TPU:0, one launch (start us, length us, event | category | flops | bytes accessed | tf_op | source)
XLA Modules:
  0.0 100.9 jit_solution(12430634139479733988)
XLA Ops:
  7.2 1.1 %copy.97 = f32[8,20,512]{2,1,0:T(8,128)S(1)} copy(bf16[8,20,512]{2,0,1:T(8,128)(2,1)} %param.10) | data formatting | bytes 491520 | tf_op jit(solution)/shard_map/convert_element_type | solution.py:55
  8.3 1.0 %multiply_reduce_fusion = f32[8,20]{0,1:T(8,128)S(1)} fusion(bf16[8,20,512]{2,0,1:T(8,128)(2,1)} %param.10), kind=kLoop, calls=%fused_computation.32 | loop fusion | flops 245600 | bytes 164480 | tf_op jit(solution)/shard_map/reduce_sum | solution.py:22
  9.6 1.5 %multiply_convert_fusion = bf16[160,512]{1,0:T(8,128)(2,1)} fusion(f32[160,512]{1,0:T(8,128)S(1)} %reshape.106, f32[512]{0:T(512)} %param.11, f32[160]{0:T(256)S(1)} %rsqrt.20), kind=kLoop, calls=%fused_computation.31 | loop fusion | flops 245760 | bytes 494208 | tf_op jit(solution)/shard_map/convert_element_type | solution.py:56
  11.0 1.2 %fusion.28 = (bf16[2,1,20,512]{3,1,2,0:T(2,128)(2,1)S(1)}, bf16[2,1,20,512]{3,1,2,0:T(2,128)(2,1)S(1)}) fusion(bf16[2,8,20,512]{3,1,2,0:T(8,128)(2,1)} %param.17), kind=kLoop, calls=%fused_computation.90 | loop fusion | bytes 163840 | tf_op jit(solution)/shard_map/slice | solution.py:13
  12.2 1.3 %collective-permute-start.1 = (bf16[2,1,20,512]{3,1,2,0:T(2,128)(2,1)S(1)}, bf16[2,1,20,512]{3,1,2,0:T(2,128)(2,1)S(1)}, u32[]{:S(2)}, u32[]{:S(2)}) collective-permute-start(bf16[2,1,20,512]{3,1,2,0:T(2,128)(2,1)S(1)} %get-tuple-element.37), channel_id=1, source_target_pairs={{4,0},{8,4},{12,8},{5,1},{9,5},{13,9},{6,2},{10,6},{14,10},{7,3},{... | collective-permute-start | bytes 122888 | tf_op jit(solution)/shard_map/ppermute | solution.py:16
  13.5 5.6 %collective-permute-start = (bf16[2,1,20,512]{3,1,2,0:T(2,128)(2,1)S(1)}, bf16[2,1,20,512]{3,1,2,0:T(2,128)(2,1)S(1)}, u32[]{:S(2)}, u32[]{:S(2)}) collective-permute-start(bf16[2,1,20,512]{3,1,2,0:T(2,128)(2,1)S(1)} %get-tuple-element.36), channel_id=1, source_target_pairs={{0,4},{4,8},{8,12},{1,5},{5,9},{9,13},{2,6},{6,10},{10,14},{3,7},{... | collective-permute-start | bytes 122888 | tf_op jit(solution)/shard_map/ppermute | solution.py:15
  19.1 1.4 %fusion.2 = bf16[160,512]{1,0:T(8,128)(2,1)S(1)} fusion(bf16[160,512]{1,0:T(8,128)(2,1)} %multiply_convert_fusion, bf16[512,512]{1,0:T(8,128)(2,1)} %param.12), kind=kOutput, calls=%fused_computation.6 | convolution fusion | flops 84049920 | bytes 851968 | tf_op jit(solution)/shard_map/dot_general | solution.py:58
  20.5 1.0 %constant_dynamic-update-slice_fusion.1 = bf16[2,9,20,512]{3,1,2,0:T(8,128)(2,1)S(1)} fusion(bf16[2,8,20,512]{3,1,2,0:T(8,128)(2,1)} %param.17), kind=kLoop, calls=%fused_computation.49 | loop fusion | bytes 655360
  21.6 0.8 pad_maximum_fusion.7
  22.3 1.3 %collective-permute-start.3 = (bf16[2,10,1,512]{3,1,2,0:T(8,128)(2,1)S(1)}, bf16[2,10,1,512]{3,1,2,0:T(8,128)(2,1)S(1)}, u32[]{:S(2)}, u32[]{:S(2)}) collective-permute-start(bf16[2,10,1,512]{3,1,2,0:T(8,128)(2,1)S(1)} %get-tuple-element.28), channel_id=1, source_target_pairs={{1,0},{2,1},{3,2},{5,4},{6,5},{7,6},{9,8},{10,9},{11,10},{13,12},{... | collective-permute-start | bytes 61448 | tf_op jit(solution)/shard_map/ppermute | solution.py:16
  23.6 3.0 %collective-permute-start.2 = (bf16[2,10,1,512]{3,1,2,0:T(8,128)(2,1)S(1)}, bf16[2,10,1,512]{3,1,2,0:T(8,128)(2,1)S(1)}, u32[]{:S(2)}, u32[]{:S(2)}) collective-permute-start(bf16[2,10,1,512]{3,1,2,0:T(8,128)(2,1)S(1)} %get-tuple-element.29), channel_id=1, source_target_pairs={{0,1},{1,2},{2,3},{4,5},{5,6},{6,7},{8,9},{9,10},{10,11},{12,13},{... | collective-permute-start | bytes 61448 | tf_op jit(solution)/shard_map/ppermute | solution.py:15
  26.7 0.1 constant_dynamic-update-slice_fusion
  26.8 0.2 fusion.27
  27.8 0.6 pad_maximum_fusion
  28.4 1.2 %fusion.24 = (bf16[1,8,20,512]{3,1,2,0:T(8,128)(2,1)}, bf16[1,8,20,512]{3,1,2,0:T(8,128)(2,1)S(1)}, bf16[1,8,20,512]{3,1,2,0:T(8,128)(2,1)S(1)}, bf16[1,8,20,512...) fusion(bf16[2,10,21,512]{3,1,2,0:T(8,128)(2,1)S(1)} %get-tuple-, ...), kind=kLoop, calls=%fused_computation.86 | loop fusion | bytes 3932160 | tf_op jit(solution)/shard_map/slice | solution.py:78
  29.7 0.7 concatenate.106
  30.4 1.0 copy.101
  31.4 1.0 copy.102
  32.3 0.7 concatenate.111
  33.0 1.0 copy.104
  34.1 0.7 concatenate.114
  35.3 1.0 copy.114
  36.3 1.6 %constant_dynamic-update-slice_fusion.31 = bf16[160,13824]{1,0:T(8,128)(2,1)} fusion(bf16[160,512]{1,0:T(8,128)(2,1)} %concatenate.106), kind=kLoop, calls=%fused_computation.79 | loop fusion | bytes 327680
  38.0 0.7 constant_dynamic-update-slice_fusion.30
  38.7 0.7 constant_dynamic-update-slice_fusion.29
  39.3 1.6 %constant_dynamic-update-slice_fusion.28 = bf16[160,13824]{1,0:T(8,128)(2,1)} fusion(bf16[160,13824]{1,0:T(8,128)(2,1)} %constant_dynamic-update-slice_fusion.29, bf16[160,512]{1,0:T(8,128)(2,1)} %concatenate.111), kind=kLoop, calls=%fused_computation.76 | loop fusion | bytes 327680
  40.9 0.7 constant_dynamic-update-slice_fusion.27
  41.7 0.7 constant_dynamic-update-slice_fusion.26
  42.4 1.6 %constant_dynamic-update-slice_fusion.25 = bf16[160,13824]{1,0:T(8,128)(2,1)} fusion(bf16[160,13824]{1,0:T(8,128)(2,1)} %constant_dynamic-update-slice_fusion.26, bf16[160,512]{1,0:T(8,128)(2,1)} %concatenate.114), kind=kLoop, calls=%fused_computation.73 | loop fusion | bytes 327680
  43.9 0.7 constant_dynamic-update-slice_fusion.24
  44.7 0.7 constant_dynamic-update-slice_fusion.23
  45.4 0.7 constant_dynamic-update-slice_fusion.22
  46.1 0.7 constant_dynamic-update-slice_fusion.21
  46.8 0.7 constant_dynamic-update-slice_fusion.20
  47.5 0.7 constant_dynamic-update-slice_fusion.19
  48.2 0.7 constant_dynamic-update-slice_fusion.18
  48.9 0.7 constant_dynamic-update-slice_fusion.17
  49.5 0.7 constant_dynamic-update-slice_fusion.16
  50.2 6.4 %all-gather.2.cloned.1.call-done = bf16[2560,512]{1,0:T(8,128)(2,1)} async-done(((bf16[160,512]{1,0:T(8,128)(2,1)}), bf16[2560,512]{1,0:T(8,128)(2,1)}) %all-gather.2.cloned.1.call-update) | async-done | bytes 2621456 | tf_op jit(solution)/shard_map/all_gather | solution.py:66
  56.6 3.1 %fusion.31 = (f32[160]{0:T(256)S(1)}, f32[160,2560]{1,0:T(8,128)S(1)}) fusion(bf16[2560,512]{1,0:T(8,128)(2,1)} %all-gather.2.cloned.1.call-done, bf16[160,512]{1,0:T(8,128)(2,1)S(1)} %fusion.2, bf16[512,512]{1,0:T(8,128)(2,1)S(1)} %copy-done), kind=kOutput, calls=%fused_computation.93 | convolution fusion | flops 503807840 | bytes 4948608 | tf_op jit(solution)/shard_map/dot_general | solution.py:28
  59.8 0.4 fusion
  60.1 3.3 %convolution_convert_fusion = bf16[160,512]{1,0:T(8,128)(2,1)} fusion(bf16[512,512]{1,0:T(8,128)(2,1)} %param.14, bf16[2560,512]{1,0:T(8,128)(2,1)} %all-gather.2.cloned.1.call-done, f32[160,2560]{1,0:T(8,128)S(1)} %get-tuple-element.55, f32[160]{0:T(256)S(1)} %broadcast_maximum_fusion, f32[160]{0:T(256)S(1)} %fusion), kind=kOutput, calls=%fused_computation.8 | convolution fusion | flops 504381440 | bytes 4949248 | tf_op jit(solution)/shard_map/dot_general | solution.py:69
  63.5 1.3 %fusion.11 = (f32[160]{0:T(256)S(1)}, bf16[160,512]{1,0:T(8,128)(2,1)S(1)}) fusion(f32[160,512]{1,0:T(8,128)S(1)} %reshape.106, bf16[160,512]{1,0:T(8,128)(2,1)} %convolution_convert_fusion, bf16[512,512]{1,0:T(8,128)(2,1)S(1)} %copy-done.3), kind=kOutput, calls=%fused_computation.23 | convolution fusion | flops 84295520 | bytes 1180288 | tf_op jit(solution)/shard_map/dot_general | solution.py:70
  64.8 0.2 fusion.18
  65.0 3.1 %collective-permute-start.4 = (bf16[1,1,20,512]{3,2,1,0:T(8,128)(2,1)S(1)}, bf16[1,1,20,512]{3,2,1,0:T(8,128)(2,1)S(1)}, u32[]{:S(2)}, u32[]{:S(2)}) collective-permute-start(bf16[1,1,20,512]{3,2,1,0:T(8,128)(2,1)S(1)} %get-tuple-element.53), channel_id=1, source_target_pairs={{0,4},{4,8},{8,12},{1,5},{5,9},{9,13},{2,6},{6,10},{10,14},{3,7},{... | collective-permute-start | bytes 61448 | tf_op jit(solution)/shard_map/ppermute | solution.py:15
  68.1 0.7 constant_dynamic-update-slice_fusion.15
  69.0 1.3 %collective-permute-start.5 = (bf16[1,1,20,512]{3,2,1,0:T(8,128)(2,1)S(1)}, bf16[1,1,20,512]{3,2,1,0:T(8,128)(2,1)S(1)}, u32[]{:S(2)}, u32[]{:S(2)}) collective-permute-start(bf16[1,1,20,512]{3,2,1,0:T(8,128)(2,1)S(1)} %get-tuple-element.52), channel_id=1, source_target_pairs={{4,0},{8,4},{12,8},{5,1},{9,5},{13,9},{6,2},{10,6},{14,10},{7,3},{... | collective-permute-start | bytes 61448 | tf_op jit(solution)/shard_map/ppermute | solution.py:16
  70.3 4.4 %collective-permute-done.5 = bf16[1,1,20,512]{3,2,1,0:T(8,128)(2,1)S(1)} collective-permute-done((bf16[1,1,20,512]{3,2,1,0:T(8,128)(2,1)S(1)}, bf16[1,1,20,512]{3,2,1,0:T(8,128)(2,1)S(1)}, u32[]{:S(2)}, u32[]{:S(2)}) %collective-permute-start.5) | collective-permute-done | bytes 20512 | tf_op jit(solution)/shard_map/ppermute | solution.py:16
  74.8 1.3 %collective-permute-start.7 = (bf16[1,10,1,512]{3,2,1,0:T(2,128)(2,1)S(1)}, bf16[1,10,1,512]{3,2,1,0:T(2,128)(2,1)S(1)}, u32[]{:S(2)}, u32[]{:S(2)}) collective-permute-start(bf16[1,10,1,512]{3,2,1,0:T(2,128)(2,1)S(1)} %get-tuple-element.47), channel_id=1, source_target_pairs={{1,0},{2,1},{3,2},{5,4},{6,5},{7,6},{9,8},{10,9},{11,10},{13,12},{... | collective-permute-start | bytes 30728 | tf_op jit(solution)/shard_map/ppermute | solution.py:16
  76.1 3.0 %collective-permute-start.6 = (bf16[1,10,1,512]{3,2,1,0:T(2,128)(2,1)S(1)}, bf16[1,10,1,512]{3,2,1,0:T(2,128)(2,1)S(1)}, u32[]{:S(2)}, u32[]{:S(2)}) collective-permute-start(bf16[1,10,1,512]{3,2,1,0:T(2,128)(2,1)S(1)} %get-tuple-element.48), channel_id=1, source_target_pairs={{0,1},{1,2},{2,3},{4,5},{5,6},{6,7},{8,9},{9,10},{10,11},{12,13},{... | collective-permute-start | bytes 30728 | tf_op jit(solution)/shard_map/ppermute | solution.py:15
  79.1 0.7 constant_dynamic-update-slice_fusion.14
  79.9 0.7 copy.117
  80.7 0.3 pad_maximum_fusion.1
  81.1 0.7 constant_dynamic-update-slice_fusion.13
  81.8 0.7 constant_dynamic-update-slice_fusion.12
  82.5 0.7 constant_dynamic-update-slice_fusion.11
  83.2 0.7 constant_dynamic-update-slice_fusion.10
  83.9 0.9 constant_dynamic-update-slice_fusion.9
  84.9 0.7 constant_dynamic-update-slice_fusion.8
  85.6 0.7 constant_dynamic-update-slice_fusion.7
  86.3 0.7 constant_dynamic-update-slice_fusion.6
  87.0 0.7 constant_dynamic-update-slice_fusion.5
  87.7 5.7 %fusion.6 = bf16[160,256]{1,0:T(8,128)(2,1)S(1)} fusion(bf16[160,13824]{1,0:T(8,128)(2,1)} %constant_dynamic-update-slice_fusion.5, bf16[13824,256]{1,0:T(8,128)(2,1)} %bitcast.12, bf16[160,512]{1,0:T(8,128)(2,1)S(1)} %get-tuple-element.57, f32[256]{0:T(256)S(1)} %copy-done.5), kind=kOutput, calls=%fused_computation.13 | convolution fusion | flops 1132625920 | bytes 11666432 | tf_op jit(solution)/shard_map/dot_general | solution.py:86
  93.4 0.7 copy.118
  (73 shorter events, 2.2 us)
Async XLA Ops:
  7.2 49.5 %copy-start = (bf16[512,512]{1,0:T(8,128)(2,1)S(1)}, bf16[512,512]{1,0:T(8,128)(2,1)}, u32[]{:S(2)}) copy-start(bf16[512,512]{1,0:T(8,128)(2,1)} %param.13) | copy-start | bytes 1572868
  7.2 19.7 %copy-start.1 = (bf16[2,8,20,512]{3,1,2,0:T(8,128)(2,1)S(1)}, bf16[2,8,20,512]{3,1,2,0:T(8,128)(2,1)}, u32[]{:S(2)}) copy-start(bf16[2,8,20,512]{3,1,2,0:T(8,128)(2,1)} %param.17) | copy-start | bytes 983044
  7.2 49.5 %all-gather.2.cloned.1.call-start = ((), (), s32[]{:S(2)}) async-start(), calls=%async_computation | async-start | bytes 2785280 | tf_op jit(solution)/shard_map/all_gather | solution.py:66
  12.2 9.3 %collective-permute-start.1 = (bf16[2,1,20,512]{3,1,2,0:T(2,128)(2,1)S(1)}, bf16[2,1,20,512]{3,1,2,0:T(2,128)(2,1)S(1)}, u32[]{:S(2)}, u32[]{:S(2)}) collective-permute-start(bf16[2,1,20,512]{3,1,2,0:T(2,128)(2,1)S(1)} %get-tuple-element.37), channel_id=1, source_target_pairs={{4,0},{8,4},{12,8},{5,1},{9,5},{13,9},{6,2},{10,6},{14,10},{7,3},{... | collective-permute-start | bytes 122888 | tf_op jit(solution)/shard_map/ppermute | solution.py:16
  13.5 8.0 %collective-permute-start = (bf16[2,1,20,512]{3,1,2,0:T(2,128)(2,1)S(1)}, bf16[2,1,20,512]{3,1,2,0:T(2,128)(2,1)S(1)}, u32[]{:S(2)}, u32[]{:S(2)}) collective-permute-start(bf16[2,1,20,512]{3,1,2,0:T(2,128)(2,1)S(1)} %get-tuple-element.36), channel_id=1, source_target_pairs={{0,4},{4,8},{8,12},{1,5},{5,9},{9,13},{2,6},{6,10},{10,14},{3,7},{... | collective-permute-start | bytes 122888 | tf_op jit(solution)/shard_map/ppermute | solution.py:15
  22.3 5.4 %collective-permute-start.3 = (bf16[2,10,1,512]{3,1,2,0:T(8,128)(2,1)S(1)}, bf16[2,10,1,512]{3,1,2,0:T(8,128)(2,1)S(1)}, u32[]{:S(2)}, u32[]{:S(2)}) collective-permute-start(bf16[2,10,1,512]{3,1,2,0:T(8,128)(2,1)S(1)} %get-tuple-element.28), channel_id=1, source_target_pairs={{1,0},{2,1},{3,2},{5,4},{6,5},{7,6},{9,8},{10,9},{11,10},{13,12},{... | collective-permute-start | bytes 61448 | tf_op jit(solution)/shard_map/ppermute | solution.py:16
  23.6 4.1 %collective-permute-start.2 = (bf16[2,10,1,512]{3,1,2,0:T(8,128)(2,1)S(1)}, bf16[2,10,1,512]{3,1,2,0:T(8,128)(2,1)S(1)}, u32[]{:S(2)}, u32[]{:S(2)}) collective-permute-start(bf16[2,10,1,512]{3,1,2,0:T(8,128)(2,1)S(1)} %get-tuple-element.29), channel_id=1, source_target_pairs={{0,1},{1,2},{2,3},{4,5},{5,6},{6,7},{8,9},{9,10},{10,11},{12,13},{... | collective-permute-start | bytes 61448 | tf_op jit(solution)/shard_map/ppermute | solution.py:15
  59.7 3.8 %copy-start.3 = (bf16[512,512]{1,0:T(8,128)(2,1)S(1)}, bf16[512,512]{1,0:T(8,128)(2,1)}, u32[]{:S(2)}) copy-start(bf16[512,512]{1,0:T(8,128)(2,1)} %param.15) | copy-start | bytes 1572868
  59.7 5.0 %copy-start.4 = (f32[512]{0:T(512)S(1)}, f32[512]{0:T(512)}, u32[]{:S(2)}) copy-start(f32[512]{0:T(512)} %param.16) | copy-start | bytes 6148
  59.7 9.1 %copy-start.2 = (bf16[1,8,20,512]{3,1,2,0:T(8,128)(2,1)S(1)}, bf16[1,8,20,512]{3,1,2,0:T(8,128)(2,1)}, u32[]{:S(2)}) copy-start(bf16[1,8,20,512]{3,1,2,0:T(8,128)(2,1)} %get-tuple-element.12) | copy-start | bytes 491524
  65.0 5.3 %collective-permute-start.4 = (bf16[1,1,20,512]{3,2,1,0:T(8,128)(2,1)S(1)}, bf16[1,1,20,512]{3,2,1,0:T(8,128)(2,1)S(1)}, u32[]{:S(2)}, u32[]{:S(2)}) collective-permute-start(bf16[1,1,20,512]{3,2,1,0:T(8,128)(2,1)S(1)} %get-tuple-element.53), channel_id=1, source_target_pairs={{0,4},{4,8},{8,12},{1,5},{5,9},{9,13},{2,6},{6,10},{10,14},{3,7},{... | collective-permute-start | bytes 61448 | tf_op jit(solution)/shard_map/ppermute | solution.py:15
  69.0 5.7 %collective-permute-start.5 = (bf16[1,1,20,512]{3,2,1,0:T(8,128)(2,1)S(1)}, bf16[1,1,20,512]{3,2,1,0:T(8,128)(2,1)S(1)}, u32[]{:S(2)}, u32[]{:S(2)}) collective-permute-start(bf16[1,1,20,512]{3,2,1,0:T(8,128)(2,1)S(1)} %get-tuple-element.52), channel_id=1, source_target_pairs={{4,0},{8,4},{12,8},{5,1},{9,5},{13,9},{6,2},{10,6},{14,10},{7,3},{... | collective-permute-start | bytes 61448 | tf_op jit(solution)/shard_map/ppermute | solution.py:16
  74.7 12.9 %copy-start.5 = (f32[256]{0:T(256)S(1)}, f32[256]{0:T(256)}, u32[]{:S(2)}) copy-start(f32[256]{0:T(256)} %param.19) | copy-start | bytes 3076
  74.8 5.9 %collective-permute-start.7 = (bf16[1,10,1,512]{3,2,1,0:T(2,128)(2,1)S(1)}, bf16[1,10,1,512]{3,2,1,0:T(2,128)(2,1)S(1)}, u32[]{:S(2)}, u32[]{:S(2)}) collective-permute-start(bf16[1,10,1,512]{3,2,1,0:T(2,128)(2,1)S(1)} %get-tuple-element.47), channel_id=1, source_target_pairs={{1,0},{2,1},{3,2},{5,4},{6,5},{7,6},{9,8},{10,9},{11,10},{13,12},{... | collective-permute-start | bytes 30728 | tf_op jit(solution)/shard_map/ppermute | solution.py:16
  76.1 4.6 %collective-permute-start.6 = (bf16[1,10,1,512]{3,2,1,0:T(2,128)(2,1)S(1)}, bf16[1,10,1,512]{3,2,1,0:T(2,128)(2,1)S(1)}, u32[]{:S(2)}, u32[]{:S(2)}) collective-permute-start(bf16[1,10,1,512]{3,2,1,0:T(2,128)(2,1)S(1)} %get-tuple-element.48), channel_id=1, source_target_pairs={{0,1},{1,2},{2,3},{4,5},{5,6},{6,7},{8,9},{9,10},{10,11},{12,13},{... | collective-permute-start | bytes 30728 | tf_op jit(solution)/shard_map/ppermute | solution.py:15
Sparse Core Ops, SparseCore 0:
  11.1 45.4 all-gather.1
where the time goes:
time: 102 us; the launch traced here: 101 us
  local copies, waits for them, and re-layouts  34.8 us (34%)
  starting transfers between devices  20 us (20%)
  matrix products  14.7 us (14%)
  between operations  14.7 us (14%)
  waiting for transfers between devices  10.8 us (11%)
  other arithmetic  5.83 us (6%)
    unnamed x41, local copies, waits for them, and re-layouts  22.5 us
    ppermute x4, starting transfers between devices, padded_2(): before = lax.ppermute(last, axis, up)  14.8 us
    all_gather x1, waiting for transfers between devices, body(): lax.all_gather(normed, ('rows', 'cols'), axis=0, tiled=True)  6.41 us
    slice x20, local copies, waits for them, and re-layouts, body(): padded[time_off, row_off:row_off + tile_rows, col_off:col_off + tile_cols...  5.93 us
    dot_general x1, matrix products, body(): jnp.dot(patches, kernel_rows, preferred_element_type=jnp.float32)  5.69 us
    ppermute x4, starting transfers between devices, padded_2(): after = lax.ppermute(first, axis, down)  5.17 us
    ppermute x4, waiting for transfers between devices, padded_2(): after = lax.ppermute(first, axis, down)  4.41 us
    concatenate x27, local copies, waits for them, and re-layouts, body(): patches = jnp.concatenate(windows, axis=-1).reshape(count, 27 * channels)  3.61 us
  transfers between devices with their start and end apart: 9, of which 2 were waited for; matrix products, arithmetic and copies ran while one was open for 30% of the time, Pallas kernels for 0%

commit v1 on v0

--- a/solution.py
+++ b/solution.py
@@ -3,6 +3,7 @@
 import jax.numpy as jnp
 from jax import lax
 from jax.sharding import PartitionSpec as P
+from jax.lax import axis_index, axis_size, ppermute
 
 
 def padded_2(value, sides, width):
@@ -60,10 +61,22 @@
     query_keys = jnp.dot(query_rows, w_key.T, preferred_element_type=jnp.float32).astype(
         jnp.bfloat16
     )
+
+    def scan_points(incoming_x, net_axis):
+        spare, x_next = (axis_size(net_axis), axis_index(net_axis))
+        mat_out, f_now = (incoming_x, 1)
+        while f_now < spare:
+            all_values = ppermute(
+                mat_out, axis_name=net_axis, perm=[(ix, ix ^ f_now) for ix in range(spare)]
+            )
+            piece_next = jnp.concatenate([mat_out, all_values], 0)
+            local_out = jnp.concatenate([all_values, mat_out], 0)
+            mat_out = jnp.where(x_next & f_now == 0, piece_next, local_out)
+            f_now = 2 * f_now
+        return mat_out
+
     final_state = fold_block(
-        start_for(count, channels),
-        query_keys,
-        lax.all_gather(normed, ("rows", "cols"), axis=0, tiled=True),
+        start_for(count, channels), query_keys, scan_points(normed, ("rows", "cols"))
     )
     pooled = (final_state[2] / final_state[1][:, None]).astype(jnp.bfloat16)
     attended = jnp.dot(pooled, w_value, preferred_element_type=jnp.float32).astype(jnp.bfloat16)

time: 102 us -> 149 us (1.46)
  waiting for transfers between devices: 10.8 us -> 51 us
  between operations: 14.7 us -> 1.26 us
  local copies, waits for them, and re-layouts: 34.8 us -> 44.9 us
  starting transfers between devices: 20 us -> 26.5 us
  other arithmetic: 5.83 us -> 8.83 us
    ppermute x0 -> x4, waiting for transfers between devices: none -> 46.5 us  [scan_points(): ppermute(mat_out, axis_name=net_axis, perm=[(ix, ix ^ f_now) for ix in ra...]
    ppermute x0 -> x4, starting transfers between devices: none -> 7.83 us  [scan_points(): ppermute(mat_out, axis_name=net_axis, perm=[(ix, ix ^ f_now) for ix in ra...]
    all_gather x1 -> x0, waiting for transfers between devices: 6.41 us -> none  [body(): lax.all_gather(normed, ('rows', 'cols'), axis=0, tiled=True)]
    slice x20, local copies, waits for them, and re-layouts: 5.93 us -> 9.71 us  [body(): padded[time_off, row_off:row_off + tile_rows, col_off:col_off + tile_cols...]
    unnamed x41 -> x43, local copies, waits for them, and re-layouts: 22.5 us -> 26.2 us
    select_n x0 -> x3, other arithmetic: none -> 3.07 us  [scan_points(): mat_out = jnp.where(x_next & f_now == 0, piece_next, local_out)]
    concatenate x27, local copies, waits for them, and re-layouts: 3.61 us -> 6.3 us  [body(): patches = jnp.concatenate(windows, axis=-1).reshape(count, 27 * channels)]
  transfers between devices with their start and end apart: 9 -> 12, of which waited for: 2 -> 4; matrix products, arithmetic and copies ran while one was open for 30% -> 28% of each run, Pallas kernels for 0% -> 0%
where the time goes in v1:
time: 149 us; the launch traced here: 148 us
  waiting for transfers between devices  51 us (34%)
  local copies, waits for them, and re-layouts  44.9 us (30%)
  starting transfers between devices  26.5 us (18%)
  matrix products  15.9 us (11%)
  other arithmetic  8.83 us (6%)
    ppermute x4, waiting for transfers between devices, scan_points(): ppermute(mat_out, axis_name=net_axis, perm=[(ix, ix ^ f_now) for ix in ra...  46.5 us
    unnamed x43, local copies, waits for them, and re-layouts  26.2 us
    ppermute x4, starting transfers between devices, padded_2(): before = lax.ppermute(last, axis, up)  13.5 us
    slice x20, local copies, waits for them, and re-layouts, body(): padded[time_off, row_off:row_off + tile_rows, col_off:col_off + tile_cols...  9.71 us
    ppermute x4, starting transfers between devices, scan_points(): ppermute(mat_out, axis_name=net_axis, perm=[(ix, ix ^ f_now) for ix in ra...  7.83 us
    concatenate x27, local copies, waits for them, and re-layouts, body(): patches = jnp.concatenate(windows, axis=-1).reshape(count, 27 * channels)  6.3 us
    dot_general x1, matrix products, body(): jnp.dot(patches, kernel_rows, preferred_element_type=jnp.float32)  5.69 us
    ppermute x4, starting transfers between devices, padded_2(): after = lax.ppermute(first, axis, down)  5.16 us
  transfers between devices with their start and end apart: 12, of which 4 were waited for; matrix products, arithmetic and copies ran while one was open for 28% of the time, Pallas kernels for 0%

profile of v1, /device:TPU:0, one launch (start us, length us, event | category | flops | bytes accessed | tf_op | source)
XLA Modules:
  0.0 148.4 jit_solution(15365356272997957105)
XLA Ops:
  0.7 1.0 copy.97
  1.7 1.0 multiply_reduce_fusion
  3.0 0.8 multiply_convert_fusion
  4.3 1.2 fusion.31
  5.5 1.3 collective-permute-start.5
  6.8 5.1 %collective-permute-start.4 = (bf16[2,1,20,512]{3,1,2,0:T(2,128)(2,1)S(1)}, bf16[2,1,20,512]{3,1,2,0:T(2,128)(2,1)S(1)}, u32[]{:S(2)}, u32[]{:S(2)}) collective-permute-start(bf16[2,1,20,512]{3,1,2,0:T(2,128)(2,1)S(1)} %get-tuple-element.36), channel_id=1, source_target_pairs={{0,4},{4,8},{8,12},{1,5},{5,9},{9,13},{2,6},{6,10},{10,14},{3,7},{... | collective-permute-start | bytes 122888 | tf_op jit(solution)/shard_map/ppermute | solution.py:16
  11.9 2.0 %fusion.2 = bf16[160,512]{1,0:T(8,128)(2,1)} fusion(bf16[160,512]{1,0:T(8,128)(2,1)S(1)} %multiply_convert_fusion, bf16[512,512]{1,0:T(8,128)(2,1)} %param.12), kind=kOutput, calls=%fused_computation.8 | convolution fusion | flops 84049920 | bytes 851968 | tf_op jit(solution)/shard_map/dot_general | solution.py:59
  13.9 1.0 constant_dynamic-update-slice_fusion.1
  14.9 1.4 pad_maximum_fusion.7
  16.3 1.3 collective-permute-start.7
  17.6 3.0 %collective-permute-start.6 = (bf16[2,10,1,512]{3,1,2,0:T(8,128)(2,1)S(1)}, bf16[2,10,1,512]{3,1,2,0:T(8,128)(2,1)S(1)}, u32[]{:S(2)}, u32[]{:S(2)}) collective-permute-start(bf16[2,10,1,512]{3,1,2,0:T(8,128)(2,1)S(1)} %get-tuple-element.29), channel_id=1, source_target_pairs={{0,1},{1,2},{2,3},{4,5},{5,6},{6,7},{8,9},{9,10},{10,11},{12,13},{... | collective-permute-start | bytes 61448 | tf_op jit(solution)/shard_map/ppermute | solution.py:16
  21.1 2.0 %collective-permute-start.1 = (bf16[320,512]{1,0:T(8,128)(2,1)S(1)}, bf16[320,512]{1,0:T(8,128)(2,1)}, u32[]{:S(2)}, u32[]{:S(2)}) collective-permute-start(bf16[320,512]{1,0:T(8,128)(2,1)S(1)} %maximum_select_fusion.6), channel_id=1, source_target_pairs={{0,2},{1,3},{2,0},{3,1},{4,6},{5,7},{6,4},{7,5},{8,10},{9,11},{10,... | collective-permute-start | bytes 983048 | tf_op jit(solution)/shard_map/ppermute | solution.py:69
  23.4 0.7 concatenate.144
  25.1 6.1 %collective-permute-done.1 = bf16[320,512]{1,0:T(8,128)(2,1)} collective-permute-done((bf16[320,512]{1,0:T(8,128)(2,1)S(1)}, bf16[320,512]{1,0:T(8,128)(2,1)}, u32[]{:S(2)}, u32[]{:S(2)}) %collective-permute-start.1) | collective-permute-done | bytes 327712 | tf_op jit(solution)/shard_map/ppermute | solution.py:69
  31.3 1.3 maximum_select_fusion.2
  32.5 2.5 %collective-permute-start.2 = (bf16[640,512]{1,0:T(8,128)(2,1)S(1)}, bf16[640,512]{1,0:T(8,128)(2,1)}, u32[]{:S(2)}, u32[]{:S(2)}) collective-permute-start(bf16[640,512]{1,0:T(8,128)(2,1)S(1)} %maximum_select_fusion.2), channel_id=1, source_target_pairs={{0,4},{1,5},{2,6},{3,7},{4,0},{5,1},{6,2},{7,3},{8,12},{9,13},{10,... | collective-permute-start | bytes 1966088 | tf_op jit(solution)/shard_map/ppermute | solution.py:69
  35.0 1.3 fusion.27
  36.6 0.7 constant_dynamic-update-slice_fusion.31
  37.4 0.7 constant_dynamic-update-slice_fusion.30
  38.7 0.7 constant_dynamic-update-slice_fusion.28
  39.5 10.6 %collective-permute-done.2 = bf16[640,512]{1,0:T(8,128)(2,1)} collective-permute-done((bf16[640,512]{1,0:T(8,128)(2,1)S(1)}, bf16[640,512]{1,0:T(8,128)(2,1)}, u32[]{:S(2)}, u32[]{:S(2)}) %collective-permute-start.2) | collective-permute-done | bytes 655392 | tf_op jit(solution)/shard_map/ppermute | solution.py:69
  50.1 1.7 %maximum_select_fusion.1 = bf16[1280,512]{1,0:T(8,128)(2,1)S(1)} fusion(bf16[640,512]{1,0:T(8,128)(2,1)} %collective-permute-done.2, bf16[640,512]{1,0:T(8,128)(2,1)S(1)} %maximum_select_fusion.2, pred[]{:T(512)S(6)} %eq.13), kind=kLoop, calls=%fused_computation.4 | loop fusion | flops 5898240 | bytes 2621441 | tf_op jit(solution)/shard_map/jit(_where)/select_n | solution.py:74
  51.8 2.8 %collective-permute-start.3 = (bf16[1280,512]{1,0:T(8,128)(2,1)S(1)}, bf16[1280,512]{1,0:T(8,128)(2,1)}, u32[]{:S(2)}, u32[]{:S(2)}) collective-permute-start(bf16[1280,512]{1,0:T(8,128)(2,1)S(1)} %maximum_select_fusion.1), channel_id=1, source_target_pairs={{0,8},{1,9},{2,10},{3,11},{4,12},{5,13},{6,14},{7,15},{8,0},{9,1},... | collective-permute-start | bytes 3932168 | tf_op jit(solution)/shard_map/ppermute | solution.py:69
  54.6 1.6 %constant_dynamic-update-slice_fusion.27 = bf16[160,13824]{1,0:T(8,128)(2,1)} fusion(bf16[160,13824]{1,0:T(8,128)(2,1)} %constant_dynamic-update-slice_fusion.28, bf16[160,512]{1,0:T(8,128)(2,1)} %concatenate.144), kind=kLoop, calls=%fused_computation.79 | loop fusion | bytes 327680
  56.3 1.0 copy.104
  57.2 0.7 concatenate.145
  57.9 1.0 copy.105
  58.9 0.7 concatenate.146
  59.6 1.0 copy.107
  60.6 0.7 concatenate.149
  61.3 1.0 copy.108
  62.3 0.7 concatenate.150
  63.0 1.0 copy.110
  64.0 1.0 copy.111
  65.0 0.7 concatenate.153
  65.7 1.0 copy.113
  66.7 1.0 copy.114
  67.6 0.7 concatenate.156
  68.3 1.6 %constant_dynamic-update-slice_fusion.26 = bf16[160,13824]{1,0:T(8,128)(2,1)} fusion(bf16[160,13824]{1,0:T(8,128)(2,1)} %constant_dynamic-update-slice_fusion.27, bf16[160,512]{1,0:T(8,128)(2,1)} %concatenate.145), kind=kLoop, calls=%fused_computation.78 | loop fusion | bytes 327680
  70.0 1.6 %constant_dynamic-update-slice_fusion.25 = bf16[160,13824]{1,0:T(8,128)(2,1)} fusion(bf16[160,13824]{1,0:T(8,128)(2,1)} %constant_dynamic-update-slice_fusion.26, bf16[160,512]{1,0:T(8,128)(2,1)} %concatenate.146), kind=kLoop, calls=%fused_computation.77 | loop fusion | bytes 327680
  72.3 1.6 %constant_dynamic-update-slice_fusion.23 = bf16[160,13824]{1,0:T(8,128)(2,1)} fusion(bf16[160,13824]{1,0:T(8,128)(2,1)} %constant_dynamic-update-slice_fusion.24, bf16[160,512]{1,0:T(8,128)(2,1)} %concatenate.149), kind=kLoop, calls=%fused_computation.75 | loop fusion | bytes 327680
  73.9 1.6 %constant_dynamic-update-slice_fusion.22 = bf16[160,13824]{1,0:T(8,128)(2,1)} fusion(bf16[160,13824]{1,0:T(8,128)(2,1)} %constant_dynamic-update-slice_fusion.23, bf16[160,512]{1,0:T(8,128)(2,1)} %concatenate.150), kind=kLoop, calls=%fused_computation.74 | loop fusion | bytes 327680
  76.1 0.7 constant_dynamic-update-slice_fusion.20
  76.8 1.6 %constant_dynamic-update-slice_fusion.19 = bf16[160,13824]{1,0:T(8,128)(2,1)} fusion(bf16[160,13824]{1,0:T(8,128)(2,1)} %constant_dynamic-update-slice_fusion.20, bf16[160,512]{1,0:T(8,128)(2,1)} %concatenate.153), kind=kLoop, calls=%fused_computation.71 | loop fusion | bytes 327680
  79.1 0.7 constant_dynamic-update-slice_fusion.17
  79.8 1.6 %constant_dynamic-update-slice_fusion.16 = bf16[160,13824]{1,0:T(8,128)(2,1)} fusion(bf16[160,13824]{1,0:T(8,128)(2,1)} %constant_dynamic-update-slice_fusion.17, bf16[160,512]{1,0:T(8,128)(2,1)} %concatenate.156), kind=kLoop, calls=%fused_computation.68 | loop fusion | bytes 327680
  81.4 29.8 %collective-permute-done.3 = bf16[1280,512]{1,0:T(8,128)(2,1)} collective-permute-done((bf16[1280,512]{1,0:T(8,128)(2,1)S(1)}, bf16[1280,512]{1,0:T(8,128)(2,1)}, u32[]{:S(2)}, u32[]{:S(2)}) %collective-permute-start.3) | collective-permute-done | bytes 1310752 | tf_op jit(solution)/shard_map/ppermute | solution.py:69
  111.2 4.0 %fusion.34 = (f32[160]{0:T(256)S(1)}, f32[160,2560]{1,0:T(8,128)S(1)}) fusion(bf16[1280,512]{1,0:T(8,128)(2,1)} %collective-permute-done.3, bf16[1280,512]{1,0:T(8,128)(2,1)} %copy-done.2, pred[]{:T(512)S(6)} %eq.12, bf16[160,512]{1,0:T(8,128)(2,1)} %fusion.2, bf16[512,512]{1,0:T(8,128)(2,1)S(1)} %copy-done), kind=kOutput, calls=%fused_computation.99 | convolution fusion | flops 515604320 | bytes 4948609 | tf_op jit(solution)/shard_map/dot_general | solution.py:29
  115.6 3.9 %convolution_convert_fusion = bf16[160,512]{1,0:T(8,128)(2,1)S(1)} fusion(bf16[512,512]{1,0:T(8,128)(2,1)} %param.14, f32[160,2560]{1,0:T(8,128)S(1)} %get-tuple-element.55, f32[160]{0:T(256)S(1)} %broadcast_maximum_fusion, bf16[1280,512]{1,0:T(8,128)(2,1)} %collective-permute-done.3, bf16[1280,512]{1,0:T(8,128)(2,1)} %copy-done.2, pred[]{:T(512)S(6)} %eq.12, ...), kind=kOutput, calls=%fused_computation.10 | convolution fusion | flops 516177920 | bytes 4949249 | tf_op jit(solution)/shard_map/dot_general | solution.py:82
  120.2 2.4 %collective-permute-start.8 = (bf16[1,1,20,512]{3,2,1,0:T(8,128)(2,1)S(1)}, bf16[1,1,20,512]{3,2,1,0:T(8,128)(2,1)S(1)}, u32[]{:S(2)}, u32[]{:S(2)}) collective-permute-start(bf16[1,1,20,512]{3,2,1,0:T(8,128)(2,1)S(1)} %get-tuple-element.53), channel_id=1, source_target_pairs={{0,4},{4,8},{8,12},{1,5},{5,9},{9,13},{2,6},{6,10},{10,14},{3,7},{... | collective-permute-start | bytes 61448 | tf_op jit(solution)/shard_map/ppermute | solution.py:16
  123.3 1.3 collective-permute-start.9
  124.7 4.4 %collective-permute-done.9 = bf16[1,1,20,512]{3,2,1,0:T(8,128)(2,1)S(1)} collective-permute-done((bf16[1,1,20,512]{3,2,1,0:T(8,128)(2,1)S(1)}, bf16[1,1,20,512]{3,2,1,0:T(8,128)(2,1)S(1)}, u32[]{:S(2)}, u32[]{:S(2)}) %collective-permute-start.9) | collective-permute-done | bytes 20512 | tf_op jit(solution)/shard_map/ppermute | solution.py:17
  129.2 1.3 collective-permute-start.11
  130.5 3.0 %collective-permute-start.10 = (bf16[1,10,1,512]{3,2,1,0:T(2,128)(2,1)S(1)}, bf16[1,10,1,512]{3,2,1,0:T(2,128)(2,1)S(1)}, u32[]{:S(2)}, u32[]{:S(2)}) collective-permute-start(bf16[1,10,1,512]{3,2,1,0:T(2,128)(2,1)S(1)} %get-tuple-element.48), channel_id=1, source_target_pairs={{0,1},{1,2},{2,3},{4,5},{5,6},{6,7},{8,9},{9,10},{10,11},{12,13},{... | collective-permute-start | bytes 30728 | tf_op jit(solution)/shard_map/ppermute | solution.py:16
  134.2 0.7 copy.117
  135.5 0.7 constant_dynamic-update-slice_fusion.13
  136.2 0.7 constant_dynamic-update-slice_fusion.12
  136.9 0.7 constant_dynamic-update-slice_fusion.11
  137.6 0.7 constant_dynamic-update-slice_fusion.10
  138.3 0.8 constant_dynamic-update-slice_fusion.9
  139.3 0.7 constant_dynamic-update-slice_fusion.8
  140.0 0.7 constant_dynamic-update-slice_fusion.7
  141.4 0.7 constant_dynamic-update-slice_fusion.5
  142.1 5.7 %fusion.6 = bf16[160,256]{1,0:T(8,128)(2,1)S(1)} fusion(bf16[160,13824]{1,0:T(8,128)(2,1)} %constant_dynamic-update-slice_fusion.5, bf16[13824,256]{1,0:T(8,128)(2,1)} %bitcast.10, bf16[160,512]{1,0:T(8,128)(2,1)S(1)} %get-tuple-element.57, f32[256]{0:T(256)S(1)} %copy-done.6), kind=kOutput, calls=%fused_computation.15 | convolution fusion | flops 1132625920 | bytes 11666432 | tf_op jit(solution)/shard_map/dot_general | solution.py:99
  (83 shorter events, 10.0 us)
Async XLA Ops:
  0.6 110.6 %copy-start = (bf16[512,512]{1,0:T(8,128)(2,1)S(1)}, bf16[512,512]{1,0:T(8,128)(2,1)}, u32[]{:S(2)}) copy-start(bf16[512,512]{1,0:T(8,128)(2,1)} %param.13) | copy-start | bytes 1572868
  0.6 20.0 %copy-start.1 = (bf16[2,8,20,512]{3,1,2,0:T(8,128)(2,1)S(1)}, bf16[2,8,20,512]{3,1,2,0:T(8,128)(2,1)}, u32[]{:S(2)}) copy-start(bf16[2,8,20,512]{3,1,2,0:T(8,128)(2,1)} %param.17) | copy-start | bytes 983044
  3.7 17.2 %collective-permute-start = (bf16[160,512]{1,0:T(8,128)(2,1)S(1)}, bf16[160,512]{1,0:T(8,128)(2,1)S(1)}, u32[]{:S(2)}, u32[]{:S(2)}) collective-permute-start(bf16[160,512]{1,0:T(8,128)(2,1)S(1)} %multiply_convert_fusion), channel_id=1, source_target_pairs={{0,1},{1,0},{2,3},{3,2},{4,5},{5,4},{6,7},{7,6},{8,9},{9,8},{10,11... | collective-permute-start | bytes 491528 | tf_op jit(solution)/shard_map/ppermute | solution.py:69
  5.5 9.4 %collective-permute-start.5 = (bf16[2,1,20,512]{3,1,2,0:T(2,128)(2,1)S(1)}, bf16[2,1,20,512]{3,1,2,0:T(2,128)(2,1)S(1)}, u32[]{:S(2)}, u32[]{:S(2)}) collective-permute-start(bf16[2,1,20,512]{3,1,2,0:T(2,128)(2,1)S(1)} %get-tuple-element.37), channel_id=1, source_target_pairs={{4,0},{8,4},{12,8},{5,1},{9,5},{13,9},{6,2},{10,6},{14,10},{7,3},{... | collective-permute-start | bytes 122888 | tf_op jit(solution)/shard_map/ppermute | solution.py:17
  6.8 8.1 %collective-permute-start.4 = (bf16[2,1,20,512]{3,1,2,0:T(2,128)(2,1)S(1)}, bf16[2,1,20,512]{3,1,2,0:T(2,128)(2,1)S(1)}, u32[]{:S(2)}, u32[]{:S(2)}) collective-permute-start(bf16[2,1,20,512]{3,1,2,0:T(2,128)(2,1)S(1)} %get-tuple-element.36), channel_id=1, source_target_pairs={{0,4},{4,8},{8,12},{1,5},{5,9},{9,13},{2,6},{6,10},{10,14},{3,7},{... | collective-permute-start | bytes 122888 | tf_op jit(solution)/shard_map/ppermute | solution.py:16
  16.3 8.1 %collective-permute-start.7 = (bf16[2,10,1,512]{3,1,2,0:T(8,128)(2,1)}, bf16[2,10,1,512]{3,1,2,0:T(8,128)(2,1)S(1)}, u32[]{:S(2)}, u32[]{:S(2)}) collective-permute-start(bf16[2,10,1,512]{3,1,2,0:T(8,128)(2,1)} %get-tuple-element.28), channel_id=1, source_target_pairs={{1,0},{2,1},{3,2},{5,4},{6,5},{7,6},{9,8},{10,9},{11,10},{13,12},{... | collective-permute-start | bytes 61448 | tf_op jit(solution)/shard_map/ppermute | solution.py:17
  17.6 6.9 %collective-permute-start.6 = (bf16[2,10,1,512]{3,1,2,0:T(8,128)(2,1)S(1)}, bf16[2,10,1,512]{3,1,2,0:T(8,128)(2,1)S(1)}, u32[]{:S(2)}, u32[]{:S(2)}) collective-permute-start(bf16[2,10,1,512]{3,1,2,0:T(8,128)(2,1)S(1)} %get-tuple-element.29), channel_id=1, source_target_pairs={{0,1},{1,2},{2,3},{4,5},{5,6},{6,7},{8,9},{9,10},{10,11},{12,13},{... | collective-permute-start | bytes 61448 | tf_op jit(solution)/shard_map/ppermute | solution.py:16
  21.1 10.2 %collective-permute-start.1 = (bf16[320,512]{1,0:T(8,128)(2,1)S(1)}, bf16[320,512]{1,0:T(8,128)(2,1)}, u32[]{:S(2)}, u32[]{:S(2)}) collective-permute-start(bf16[320,512]{1,0:T(8,128)(2,1)S(1)} %maximum_select_fusion.6), channel_id=1, source_target_pairs={{0,2},{1,3},{2,0},{3,1},{4,6},{5,7},{6,4},{7,5},{8,10},{9,11},{10,... | collective-permute-start | bytes 983048 | tf_op jit(solution)/shard_map/ppermute | solution.py:69
  32.5 17.6 %collective-permute-start.2 = (bf16[640,512]{1,0:T(8,128)(2,1)S(1)}, bf16[640,512]{1,0:T(8,128)(2,1)}, u32[]{:S(2)}, u32[]{:S(2)}) collective-permute-start(bf16[640,512]{1,0:T(8,128)(2,1)S(1)} %maximum_select_fusion.2), channel_id=1, source_target_pairs={{0,4},{1,5},{2,6},{3,7},{4,0},{5,1},{6,2},{7,3},{8,12},{9,13},{10,... | collective-permute-start | bytes 1966088 | tf_op jit(solution)/shard_map/ppermute | solution.py:69
  51.8 27.3 %copy-start.2 = (bf16[1280,512]{1,0:T(8,128)(2,1)}, bf16[1280,512]{1,0:T(8,128)(2,1)S(1)}, u32[]{:S(2)}) copy-start(bf16[1280,512]{1,0:T(8,128)(2,1)S(1)} %maximum_select_fusion.1) | copy-start | bytes 3932164
  51.8 59.4 %collective-permute-start.3 = (bf16[1280,512]{1,0:T(8,128)(2,1)S(1)}, bf16[1280,512]{1,0:T(8,128)(2,1)}, u32[]{:S(2)}, u32[]{:S(2)}) collective-permute-start(bf16[1280,512]{1,0:T(8,128)(2,1)S(1)} %maximum_select_fusion.1), channel_id=1, source_target_pairs={{0,8},{1,9},{2,10},{3,11},{4,12},{5,13},{6,14},{7,15},{8,0},{9,1},... | collective-permute-start | bytes 3932168 | tf_op jit(solution)/shard_map/ppermute | solution.py:69
  115.6 4.0 %copy-start.4 = (bf16[512,512]{1,0:T(8,128)(2,1)S(1)}, bf16[512,512]{1,0:T(8,128)(2,1)}, u32[]{:S(2)}) copy-start(bf16[512,512]{1,0:T(8,128)(2,1)} %param.15) | copy-start | bytes 1572868
  115.6 4.3 %copy-start.5 = (f32[512]{0:T(512)S(1)}, f32[512]{0:T(512)}, u32[]{:S(2)}) copy-start(f32[512]{0:T(512)} %param.16) | copy-start | bytes 6148
  115.6 7.6 %copy-start.3 = (bf16[1,8,20,512]{3,1,2,0:T(8,128)(2,1)S(1)}, bf16[1,8,20,512]{3,1,2,0:T(8,128)(2,1)}, u32[]{:S(2)}) copy-start(bf16[1,8,20,512]{3,1,2,0:T(8,128)(2,1)} %get-tuple-element.12) | copy-start | bytes 491524
  120.2 4.5 %collective-permute-start.8 = (bf16[1,1,20,512]{3,2,1,0:T(8,128)(2,1)S(1)}, bf16[1,1,20,512]{3,2,1,0:T(8,128)(2,1)S(1)}, u32[]{:S(2)}, u32[]{:S(2)}) collective-permute-start(bf16[1,1,20,512]{3,2,1,0:T(8,128)(2,1)S(1)} %get-tuple-element.53), channel_id=1, source_target_pairs={{0,4},{4,8},{8,12},{1,5},{5,9},{9,13},{2,6},{6,10},{10,14},{3,7},{... | collective-permute-start | bytes 61448 | tf_op jit(solution)/shard_map/ppermute | solution.py:16
  123.3 5.7 %collective-permute-start.9 = (bf16[1,1,20,512]{3,2,1,0:T(8,128)(2,1)S(1)}, bf16[1,1,20,512]{3,2,1,0:T(8,128)(2,1)S(1)}, u32[]{:S(2)}, u32[]{:S(2)}) collective-permute-start(bf16[1,1,20,512]{3,2,1,0:T(8,128)(2,1)S(1)} %get-tuple-element.52), channel_id=1, source_target_pairs={{4,0},{8,4},{12,8},{5,1},{9,5},{13,9},{6,2},{10,6},{14,10},{7,3},{... | collective-permute-start | bytes 61448 | tf_op jit(solution)/shard_map/ppermute | solution.py:17
  129.1 12.9 %copy-start.6 = (f32[256]{0:T(256)S(1)}, f32[256]{0:T(256)}, u32[]{:S(2)}) copy-start(f32[256]{0:T(256)} %param.19) | copy-start | bytes 3076
  129.2 5.9 %collective-permute-start.11 = (bf16[1,10,1,512]{3,2,1,0:T(2,128)(2,1)S(1)}, bf16[1,10,1,512]{3,2,1,0:T(2,128)(2,1)S(1)}, u32[]{:S(2)}, u32[]{:S(2)}) collective-permute-start(bf16[1,10,1,512]{3,2,1,0:T(2,128)(2,1)S(1)} %get-tuple-element.47), channel_id=1, source_target_pairs={{1,0},{2,1},{3,2},{5,4},{6,5},{7,6},{9,8},{10,9},{11,10},{13,12},{... | collective-permute-start | bytes 30728 | tf_op jit(solution)/shard_map/ppermute | solution.py:17
  130.5 4.6 %collective-permute-start.10 = (bf16[1,10,1,512]{3,2,1,0:T(2,128)(2,1)S(1)}, bf16[1,10,1,512]{3,2,1,0:T(2,128)(2,1)S(1)}, u32[]{:S(2)}, u32[]{:S(2)}) collective-permute-start(bf16[1,10,1,512]{3,2,1,0:T(2,128)(2,1)S(1)} %get-tuple-element.48), channel_id=1, source_target_pairs={{0,1},{1,2},{2,3},{4,5},{5,6},{6,7},{8,9},{9,10},{10,11},{12,13},{... | collective-permute-start | bytes 30728 | tf_op jit(solution)/shard_map/ppermute | solution.py:16
